TPU v7x, 32 devices: a whole 2x2x4 slice. The times are simulated.
32 devices in a mesh: ctx: 4 (over y, x), wsh: 8 (over z, core).
Axes of the slice: x: 2, y: 2, z: 4, core: 2. Of those that a mesh axis runs over, the one named last changes fastest.
Arguments:
- tokens: bfloat16 [8, 2048, 768], P('wsh', 'ctx'), may hold values from -6 to 6
- cluster_order: int32 [8, 2048], P('wsh', 'ctx'), may hold values from 0 to 2047, as said below
- qkv_weight: bfloat16 [768, 2304], P('wsh'), may hold values from -0.21875 to 0.21875
- query_bias: bfloat16 [768], P('wsh'), may hold values from -3 to 3
- value_bias: bfloat16 [768], P('wsh'), may hold values from -1.25 to 1.25
- out_weight: bfloat16 [768, 768], P('wsh'), may hold values from -1.25 to 1.25
- out_bias: bfloat16 [768], P('wsh'), may hold values from -1.75 to 1.75
- first_gain: bfloat16 [768], P('wsh'), may hold values from 0.25 to 1.75
- first_shift: bfloat16 [768], P('wsh'), may hold values from -1.75 to 1.75
- up_weight: bfloat16 [768, 3072], P('wsh'), may hold values from -0.21875 to 0.21875
- up_bias: bfloat16 [3072], P('wsh'), may hold values from -3 to 3
- down_weight: bfloat16 [3072, 768], P('wsh'), may hold values from -0.109375 to 0.109375
- down_bias: bfloat16 [768], P('wsh'), may hold values from -1.75 to 1.75
- second_gain: bfloat16 [768], P('wsh'), may hold values from 0.25 to 1.75
- second_shift: bfloat16 [768], P('wsh'), may hold values from -1.75 to 1.75
- cotangent: bfloat16 [8, 2048, 768], P('wsh', 'ctx'), may hold values from -6 to 6
Outputs:
- layer_out: bfloat16 [8, 2048, 768], P('wsh', 'ctx')
- grad_tokens: float32 [8, 2048, 768], P('wsh', 'ctx')
- grad_qkv_weight: float32 [768, 2304], P('wsh')
- grad_query_bias: float32 [768], P('wsh')
- grad_value_bias: float32 [768], P('wsh')
- grad_out_weight: float32 [768, 768], P('wsh')
- grad_out_bias: float32 [768], P('wsh')
- grad_first_gain: float32 [768], P('wsh')
- grad_first_shift: float32 [768], P('wsh')
- grad_up_weight: float32 [768, 3072], P('wsh')
- grad_up_bias: float32 [3072], P('wsh')
- grad_down_weight: float32 [3072, 768], P('wsh')
- grad_down_bias: float32 [768], P('wsh')
- grad_second_gain: float32 [768], P('wsh')
- grad_second_shift: float32 [768], P('wsh')
Inputs may be any that keep to these rules, and one draw needn't show every extreme that they name: `cluster_order`: each stream's row is a permutation of its positions. The stream is cut into four documents, each a multiple of 128 tokens long, the longest exactly 1024; the permutation maps every document's positions onto themselves, so each cluster lies within one document.
All inputs are finite; a program needn't handle non-finite values.
Results may differ from a plain program's by a relative error of at most 0.02.
Values may be sent and summed in bfloat16 or wider, within the bound.
A program may use at most 128 MiB of HBM per device.

v0:
```python
import jax
import jax.numpy as jnp
from jax import lax
from jax.sharding import PartitionSpec as P

HEAD_DIM = 64
CLUSTER = 128
epsilon = 1e-05


def inner(left, right):
    return lax.dot_general(
        left, right, (((0,), (0,)), ((), ())), preferred_element_type=jnp.float32
    )


def times_transposed(left, right):
    return lax.dot_general(
        left, right, (((1,), (1,)), ((), ())), preferred_element_type=jnp.float32
    )


def normalize(values):
    centre = values - jnp.mean(values, axis=1, keepdims=True)
    factor = lax.rsqrt(jnp.mean(centre * centre, axis=1, keepdims=True) + epsilon)
    return (centre * factor, factor)


def norm_back(grad_out, normed, factor, gain):
    grad_normed = grad_out * gain
    return factor * (
        grad_normed
        - jnp.mean(grad_normed, axis=1, keepdims=True)
        - normed * jnp.mean(grad_normed * normed, axis=1, keepdims=True)
    )


def on_device(
    tokens,
    cluster_order,
    qkv_weight,
    query_bias,
    value_bias,
    out_weight,
    out_bias,
    first_gain,
    first_shift,
    up_weight,
    up_bias,
    down_weight,
    down_bias,
    second_gain,
    second_shift,
    cotangent,
):
    inputs = tokens[0]
    order = cluster_order[0]
    rows = inputs.shape[0]
    width = inputs.shape[1]
    heads = width // HEAD_DIM
    blocks = rows // CLUSTER
    group_rows = rows * lax.axis_size("ctx")
    factor_qk = HEAD_DIM ** (-0.5)
    (
        whole_qkv,
        whole_qbias,
        whole_vbias,
        whole_out,
        whole_obias,
        whole_gain1,
        whole_shift1,
        whole_up,
        whole_ubias,
        whole_down,
        whole_dbias,
        whole_gain2,
        whole_shift2,
    ) = (
        lax.all_gather(qkv_weight, "wsh", axis=0, tiled=True),
        lax.all_gather(query_bias, "wsh", axis=0, tiled=True),
        lax.all_gather(value_bias, "wsh", axis=0, tiled=True),
        lax.all_gather(out_weight, "wsh", axis=0, tiled=True),
        lax.all_gather(out_bias, "wsh", axis=0, tiled=True),
        lax.all_gather(first_gain, "wsh", axis=0, tiled=True),
        lax.all_gather(first_shift, "wsh", axis=0, tiled=True),
        lax.all_gather(up_weight, "wsh", axis=0, tiled=True),
        lax.all_gather(up_bias, "wsh", axis=0, tiled=True),
        lax.all_gather(down_weight, "wsh", axis=0, tiled=True),
        lax.all_gather(down_bias, "wsh", axis=0, tiled=True),
        lax.all_gather(second_gain, "wsh", axis=0, tiled=True),
        lax.all_gather(second_shift, "wsh", axis=0, tiled=True),
    )
    qkv_shift = jnp.concatenate(
        [
            whole_qbias.astype(jnp.float32),
            jnp.zeros((width,), jnp.float32),
            whole_vbias.astype(jnp.float32),
        ]
    )
    out_shift = whole_obias.astype(jnp.float32)
    gain_one = whole_gain1.astype(jnp.float32)
    shift_one = whole_shift1.astype(jnp.float32)
    up_shift = whole_ubias.astype(jnp.float32)
    down_shift = whole_dbias.astype(jnp.float32)
    gain_two = whole_gain2.astype(jnp.float32)
    shift_two = whole_shift2.astype(jnp.float32)
    own_qkv = (jnp.dot(inputs, whole_qkv, preferred_element_type=jnp.float32) + qkv_shift).astype(
        jnp.bfloat16
    )
    group_qkv = lax.all_gather(own_qkv, "ctx", axis=0, tiled=True)
    picked = jnp.take(group_qkv, order, axis=0)
    query = picked[:, :width].reshape(blocks, CLUSTER, heads, HEAD_DIM)
    keyed = picked[:, width : 2 * width].reshape(blocks, CLUSTER, heads, HEAD_DIM)
    valued = picked[:, 2 * width :].reshape(blocks, CLUSTER, heads, HEAD_DIM)
    places = order.reshape(blocks, CLUSTER)
    visible = (places[:, None, :] <= places[:, :, None])[:, None, :, :]
    scores = (
        jnp.einsum("cihd,cjhd->chij", query, keyed, preferred_element_type=jnp.float32) * factor_qk
    )
    masked = jnp.where(visible, scores, -1e30)
    row_max = jnp.max(masked, axis=3, keepdims=True)
    expd = jnp.where(visible, jnp.exp(masked - row_max), 0.0)
    total = jnp.sum(expd, axis=3, keepdims=True)
    log_total = row_max + jnp.log(total)
    probs = (expd / total).astype(jnp.bfloat16)
    context = (
        jnp.einsum("chij,cjhd->cihd", probs, valued, preferred_element_type=jnp.float32)
        .astype(jnp.bfloat16)
        .reshape(rows, width)
    )
    branch = (jnp.dot(context, whole_out, preferred_element_type=jnp.float32) + out_shift).astype(
        jnp.bfloat16
    )
    spread = jnp.zeros((group_rows, width), jnp.bfloat16).at[order].set(branch)
    attended = lax.psum_scatter(spread, "ctx", scatter_dimension=0, tiled=True).astype(jnp.float32)
    resid = inputs.astype(jnp.float32) + attended
    first_norm, first_factor = normalize(resid)
    first_out = first_norm * gain_one + shift_one
    first_low = first_out.astype(jnp.bfloat16)
    pre_act = jnp.dot(first_low, whole_up, preferred_element_type=jnp.float32) + up_shift
    hidden = jax.nn.gelu(pre_act, approximate=False).astype(jnp.bfloat16)
    second_in = (
        first_out + jnp.dot(hidden, whole_down, preferred_element_type=jnp.float32) + down_shift
    )
    second_norm, second_factor = normalize(second_in)
    layer_out = (second_norm * gain_two + shift_two).astype(jnp.bfloat16)
    grad_top = cotangent[0].astype(jnp.float32)
    grad_gain_two = jnp.sum(grad_top * second_norm, axis=0)
    grad_shift_two = jnp.sum(grad_top, axis=0)
    grad_second = norm_back(grad_top, second_norm, second_factor, gain_two)
    grad_branch2 = grad_second.astype(jnp.bfloat16)
    grad_down_w = inner(hidden, grad_branch2)
    grad_down_b = jnp.sum(grad_branch2.astype(jnp.float32), axis=0)
    grad_hidden = times_transposed(grad_branch2, whole_down)
    slope = (
        0.5 * (1.0 + lax.erf(pre_act * 0.7071067811865476))
        + pre_act * jnp.exp(-0.5 * pre_act * pre_act) * 0.3989422804014327
    )
    grad_pre = (grad_hidden * slope).astype(jnp.bfloat16)
    grad_up_w = inner(first_low, grad_pre)
    grad_up_b = jnp.sum(grad_pre.astype(jnp.float32), axis=0)
    grad_first = grad_second + times_transposed(grad_pre, whole_up)
    grad_gain_one = jnp.sum(grad_first * first_norm, axis=0)
    grad_shift_one = jnp.sum(grad_first, axis=0)
    grad_resid = norm_back(grad_first, first_norm, first_factor, gain_one)
    grad_attended = grad_resid.astype(jnp.bfloat16)
    grad_out_b = jnp.sum(grad_attended.astype(jnp.float32), axis=0)
    group_grads = lax.all_gather(grad_attended, "ctx", axis=0, tiled=True)
    picked_grad = jnp.take(group_grads, order, axis=0)
    grad_out_w = inner(context, picked_grad)
    grad_context = (
        times_transposed(picked_grad, whole_out)
        .astype(jnp.bfloat16)
        .reshape(blocks, CLUSTER, heads, HEAD_DIM)
    )
    again = (
        jnp.einsum("cihd,cjhd->chij", query, keyed, preferred_element_type=jnp.float32) * factor_qk
    )
    probs_full = jnp.where(visible, jnp.exp(jnp.where(visible, again, -1e30) - log_total), 0.0)
    probs_low = probs_full.astype(jnp.bfloat16)
    grad_probs = jnp.einsum(
        "cihd,cjhd->chij", grad_context, valued, preferred_element_type=jnp.float32
    )
    grad_valued = jnp.einsum(
        "chij,cihd->cjhd", probs_low, grad_context, preferred_element_type=jnp.float32
    ).astype(jnp.bfloat16)
    inner_sum = jnp.sum(probs_full * grad_probs, axis=3, keepdims=True)
    grad_scores = (probs_full * (grad_probs - inner_sum)).astype(jnp.bfloat16)
    grad_query = (
        jnp.einsum("chij,cjhd->cihd", grad_scores, keyed, preferred_element_type=jnp.float32)
        * factor_qk
    ).astype(jnp.bfloat16)
    grad_keyed = (
        jnp.einsum("chij,cihd->cjhd", grad_scores, query, preferred_element_type=jnp.float32)
        * factor_qk
    ).astype(jnp.bfloat16)
    grad_picked = jnp.concatenate(
        [
            grad_query.reshape(rows, width),
            grad_keyed.reshape(rows, width),
            grad_valued.reshape(rows, width),
        ],
        axis=1,
    )
    grad_query_b = jnp.sum(grad_picked[:, :width].astype(jnp.float32), axis=0)
    grad_value_b = jnp.sum(grad_picked[:, 2 * width :].astype(jnp.float32), axis=0)
    spread_grad = jnp.zeros((group_rows, 3 * width), jnp.bfloat16).at[order].set(grad_picked)
    own_grad = (
        lax.psum_scatter(spread_grad, "ctx", scatter_dimension=0, tiled=True)
        .astype(jnp.float32)
        .astype(jnp.bfloat16)
    )
    grad_qkv_w = inner(inputs, own_grad)
    grad_inputs = grad_resid + times_transposed(own_grad, whole_qkv)
    totals = (
        lax.psum_scatter(
            grad_qkv_w.astype(jnp.bfloat16), "wsh", scatter_dimension=0, tiled=True
        ).astype(jnp.float32),
        lax.psum_scatter(
            grad_query_b.astype(jnp.bfloat16), "wsh", scatter_dimension=0, tiled=True
        ).astype(jnp.float32),
        lax.psum_scatter(
            grad_value_b.astype(jnp.bfloat16), "wsh", scatter_dimension=0, tiled=True
        ).astype(jnp.float32),
        lax.psum_scatter(
            grad_out_w.astype(jnp.bfloat16), "wsh", scatter_dimension=0, tiled=True
        ).astype(jnp.float32),
        lax.psum_scatter(
            grad_out_b.astype(jnp.bfloat16), "wsh", scatter_dimension=0, tiled=True
        ).astype(jnp.float32),
        lax.psum_scatter(
            grad_gain_one.astype(jnp.bfloat16), "wsh", scatter_dimension=0, tiled=True
        ).astype(jnp.float32),
        lax.psum_scatter(
            grad_shift_one.astype(jnp.bfloat16), "wsh", scatter_dimension=0, tiled=True
        ).astype(jnp.float32),
        lax.psum_scatter(
            grad_up_w.astype(jnp.bfloat16), "wsh", scatter_dimension=0, tiled=True
        ).astype(jnp.float32),
        lax.psum_scatter(
            grad_up_b.astype(jnp.bfloat16), "wsh", scatter_dimension=0, tiled=True
        ).astype(jnp.float32),
        lax.psum_scatter(
            grad_down_w.astype(jnp.bfloat16), "wsh", scatter_dimension=0, tiled=True
        ).astype(jnp.float32),
        lax.psum_scatter(
            grad_down_b.astype(jnp.bfloat16), "wsh", scatter_dimension=0, tiled=True
        ).astype(jnp.float32),
        lax.psum_scatter(
            grad_gain_two.astype(jnp.bfloat16), "wsh", scatter_dimension=0, tiled=True
        ).astype(jnp.float32),
        lax.psum_scatter(
            grad_shift_two.astype(jnp.bfloat16), "wsh", scatter_dimension=0, tiled=True
        ).astype(jnp.float32),
    )
    (
        sum_qkv,
        sum_qbias,
        sum_vbias,
        sum_out,
        sum_obias,
        sum_gain1,
        sum_shift1,
        sum_up,
        sum_ubias,
        sum_down,
        sum_dbias,
        sum_gain2,
        sum_shift2,
    ) = (
        lax.psum(totals[0].astype(jnp.bfloat16), "ctx").astype(jnp.float32),
        lax.psum(totals[1].astype(jnp.bfloat16), "ctx").astype(jnp.float32),
        lax.psum(totals[2].astype(jnp.bfloat16), "ctx").astype(jnp.float32),
        lax.psum(totals[3].astype(jnp.bfloat16), "ctx").astype(jnp.float32),
        lax.psum(totals[4].astype(jnp.bfloat16), "ctx").astype(jnp.float32),
        lax.psum(totals[5].astype(jnp.bfloat16), "ctx").astype(jnp.float32),
        lax.psum(totals[6].astype(jnp.bfloat16), "ctx").astype(jnp.float32),
        lax.psum(totals[7].astype(jnp.bfloat16), "ctx").astype(jnp.float32),
        lax.psum(totals[8].astype(jnp.bfloat16), "ctx").astype(jnp.float32),
        lax.psum(totals[9].astype(jnp.bfloat16), "ctx").astype(jnp.float32),
        lax.psum(totals[10].astype(jnp.bfloat16), "ctx").astype(jnp.float32),
        lax.psum(totals[11].astype(jnp.bfloat16), "ctx").astype(jnp.float32),
        lax.psum(totals[12].astype(jnp.bfloat16), "ctx").astype(jnp.float32),
    )
    return (
        layer_out[None],
        grad_inputs[None],
        sum_qkv,
        sum_qbias,
        sum_vbias,
        sum_out,
        sum_obias,
        sum_gain1,
        sum_shift1,
        sum_up,
        sum_ubias,
        sum_down,
        sum_dbias,
        sum_gain2,
        sum_shift2,
    )


def solution(mesh):
    in_specs = (
        P("wsh", "ctx", None),
        P("wsh", "ctx"),
        P("wsh", None),
        P("wsh"),
        P("wsh"),
        P("wsh", None),
        P("wsh"),
        P("wsh"),
        P("wsh"),
        P("wsh", None),
        P("wsh"),
        P("wsh", None),
        P("wsh"),
        P("wsh"),
        P("wsh"),
        P("wsh", "ctx", None),
    )
    out_specs = (
        P("wsh", "ctx", None),
        P("wsh", "ctx", None),
        P("wsh", None),
        P("wsh"),
        P("wsh"),
        P("wsh", None),
        P("wsh"),
        P("wsh"),
        P("wsh"),
        P("wsh", None),
        P("wsh"),
        P("wsh", None),
        P("wsh"),
        P("wsh"),
        P("wsh"),
    )
    return jax.shard_map(
        on_device, mesh=mesh, in_specs=in_specs, out_specs=out_specs, check_vma=False
    )
```

profile of v0, /device:TPU:0, one launch (start us, length us, event | category | flops | bytes accessed | tf_op | source)
XLA Modules:
  0.0 820.0 jit_solution(3565493798486074965)
XLA Ops:
  8.0 1.3 fusion.86
  15.8 31.6 %all-reduce.18 = (bf16[768]{0:T(1024)(128)(2,1)S(1)}, bf16[768]{0:T(1024)(128)(2,1)S(1)}, bf16[768]{0:T(1024)(128)(2,1)S(1)}, bf16[768]{0:T(1024)(128)(2,1)S(1)}...) all-reduce(bf16[768]{0:T(1024)(128)(2,1)S(1)} %dynamic-update-slice, ...), channel_id=1, replica_groups=mesh['ctx'=4,'wsh'=8] {'wsh'}, use_global_device_ids=true, to_apply=%add.1 | all-reduce | flops 5376 | bytes 21504
  47.5 7.0 all-gather.8.cloned.1.call-done
  54.4 5.6 fusion.18
  61.1 94.4 %all-gather.10.cloned.1.call-done = bf16[2048,2304]{1,0:T(8,128)(2,1)} async-done(((bf16[512,2304]{1,0:T(8,128)(2,1)}), bf16[2048,2304]{1,0:T(8,128)(2,1)}) %all-gather.10.cloned.1.call-update) | async-done | bytes 9437200 | tf_op jit(solution)/shard_map/all_gather | solution.py:110
  155.5 10.8 %gather_fusion = bf16[512,2304]{1,0:T(8,128)(2,1)} fusion(bf16[2048,2304]{1,0:T(8,128)(2,1)} %all-gather.10.cloned.1.call-done, s32[1024]{0:T(1024)S(1)} %pad_clamp_fusion), kind=kCustom, calls=%fused_computation | custom fusion | bytes 4720640 | tf_op jit(solution)/shard_map/jit(_take)/gather | solution.py:111
  166.3 1.9 broadcast_select_fusion
  175.8 4.1 all-gather.12.cloned.1.call-done
  179.8 2.1 add_convert_fusion.1
  182.0 4.7 scatter_custom_fusion
  187.9 13.1 %all-gather = bf16[8,1,384]{2,1,0:T(2,128)(2,1)S(1)} all-gather(bf16[1,1,384]{2,1,0:T(2,128)(2,1)S(1)} %reshape.219), channel_id=1, replica_groups=mesh['ctx'=4,'wsh'=8] {'wsh'}, dimensions={0}, use_global_device_ids=true | all-gather | bytes 6912 | tf_op jit(solution)/shard_map/all_gather | solution.py:87
  201.1 29.5 %reduce-scatter.9.cloned.1.call-done = bf16[512,768]{1,0:T(8,128)(2,1)} async-done(((bf16[2048,768]{1,0:T(8,128)(2,1)}), bf16[512,768]{1,0:T(8,128)(2,1)}) %reduce-scatter.9.cloned.1.call-update) | async-done | bytes 786448 | tf_op jit(solution)/shard_map/reduce_scatter | solution.py:135
  230.6 1.5 fusion.36
  232.1 1.5 multiply_reduce_fusion.4
  233.6 50.2 %all-gather.14.cloned.1.call-done = bf16[768,3072]{1,0:T(8,128)(2,1)} async-done(((bf16[96,3072]{1,0:T(8,128)(2,1)}), bf16[768,3072]{1,0:T(8,128)(2,1)}) %all-gather.14.cloned.1.call-update) | async-done | bytes 4718608 | tf_op jit(solution)/shard_map/all_gather | solution.py:86
  283.8 19.3 %fusion.2 = (bf16[512,3072]{1,0:T(8,128)(2,1)}, f32[512,3072]{1,0:T(8,128)}) fusion(f32[3072]{0:T(1024)S(1)} %bitcast.121, bf16[768,3072]{1,0:T(8,128)(2,1)} %all-gather.14.cloned.1.call-done, f32[768]{0:T(1024)S(1)} %convert_element_type.212, f32[768]{0:T(1024)S(1)} %convert_element_type.211, f32[512]{0:T(512)S(1)} %add_rsqrt_fusion.1, ...), kind=kOutput, calls=%fused_computation.8 | convolution fusion | flops 2522873856 | bytes 15751168 | tf_op jit(solution)/shard_map/dot_general | solution.py:140
  303.1 32.7 %all-gather.16.cloned.1.call-done = bf16[3072,768]{1,0:T(8,128)(2,1)} async-done(((bf16[384,768]{1,0:T(8,128)(2,1)}), bf16[3072,768]{1,0:T(8,128)(2,1)}) %all-gather.16.cloned.1.call-update) | async-done | bytes 4718608 | tf_op jit(solution)/shard_map/all_gather | solution.py:88
  335.8 6.3 fusion.87
  344.8 4.7 fusion.90
  349.6 3.2 multiply_reduce_fusion.1
  354.0 1.5 fusion.83
  355.6 42.9 %all-gather.18.cloned.1.call-done = bf16[2048,768]{1,0:T(8,128)(2,1)} async-done(((bf16[512,768]{1,0:T(8,128)(2,1)}), bf16[2048,768]{1,0:T(8,128)(2,1)}) %all-gather.18.cloned.1.call-update) | async-done | bytes 3145744 | tf_op jit(solution)/shard_map/all_gather | solution.py:168
  398.5 5.5 gather_fusion.1
  404.0 3.2 convolution_convert_fusion.4
  407.2 2.3 copy.89
  409.5 2.4 reshape.158
  412.0 3.8 multiply_reduce_fusion
  422.9 1.7 pad_maximum_fusion
  424.6 4.3 copy.101
  428.9 10.7 %scatter_custom_fusion.1 = bf16[2048,2304]{1,0:T(8,128)(2,1)} fusion(s32[512]{0:T(512)S(1)} %bitcast.125, bf16[512,2304]{1,0:T(8,128)(2,1)} %copy.101, bf16[]{:T(256)} %constant.42.clone.1), kind=kCustom, calls=%fused_computation.34 | custom fusion | bytes 9437696 | tf_op jit(solution)/shard_map/scatter | solution.py:207
  439.7 95.1 %reduce-scatter.11.cloned.1.call-done = bf16[512,2304]{1,0:T(8,128)(2,1)} async-done(((bf16[2048,2304]{1,0:T(8,128)(2,1)}), bf16[512,2304]{1,0:T(8,128)(2,1)}) %reduce-scatter.11.cloned.1.call-update) | async-done | bytes 2359312 | tf_op jit(solution)/shard_map/reduce_scatter | solution.py:209
  534.8 5.5 fusion.19
  540.3 5.8 copy.107
  546.2 3.3 convolution_convert_fusion.3
  549.5 6.5 convolution_convert_fusion.1
  556.3 7.2 convolution_convert_fusion
  563.6 26.5 %reduce-scatter.19.cloned.1.call-done = bf16[96,2304]{1,0:T(8,128)(2,1)} async-done(((bf16[768,2304]{1,0:T(8,128)(2,1)}), bf16[96,2304]{1,0:T(8,128)(2,1)}) %reduce-scatter.19.cloned.1.call-update) | async-done | bytes 442384
  590.1 2.1 copy.108
  592.2 32.2 %reduce-scatter.13.cloned.1.call-done = bf16[96,768]{1,0:T(8,128)(2,1)} async-done(((bf16[768,768]{1,0:T(8,128)(2,1)}), bf16[96,768]{1,0:T(8,128)(2,1)}) %reduce-scatter.13.cloned.1.call-update) | async-done | bytes 147472 | tf_op jit(solution)/shard_map/reduce_scatter | solution.py:225
  624.3 55.5 %reduce-scatter.15.cloned.1.call-done = bf16[96,3072]{1,0:T(8,128)(2,1)} async-done(((bf16[768,3072]{1,0:T(8,128)(2,1)}), bf16[96,3072]{1,0:T(8,128)(2,1)}) %reduce-scatter.15.cloned.1.call-update) | async-done | bytes 589840 | tf_op jit(solution)/shard_map/reduce_scatter | solution.py:237
  679.8 55.6 %reduce-scatter.17.cloned.1.call-done = bf16[384,768]{1,0:T(8,128)(2,1)} async-done(((bf16[3072,768]{1,0:T(8,128)(2,1)}), bf16[384,768]{1,0:T(8,128)(2,1)}) %reduce-scatter.17.cloned.1.call-update) | async-done | bytes 589840 | tf_op jit(solution)/shard_map/reduce_scatter | solution.py:243
  738.4 26.0 %all-reduce.17 = (bf16[768]{0:T(1024)(128)(2,1)S(1)}, bf16[768]{0:T(1024)(128)(2,1)S(1)}, bf16[768]{0:T(1024)(128)(2,1)S(1)}, bf16[768]{0:T(1024)(128)(2,1)S(1)}...) all-reduce(bf16[768]{0:T(1024)(128)(2,1)S(1)} %dynamic-update-slice, ...), channel_id=1, replica_groups=mesh['ctx'=4,'wsh'=8] {'wsh'}, use_global_device_ids=true, to_apply=%add.7 | all-reduce | flops 9984 | bytes 39936
  765.1 9.9 %all-reduce.19 = (bf16[96]{0:T(256)(128)(2,1)S(1)}, bf16[96]{0:T(256)(128)(2,1)S(1)}, bf16[96]{0:T(256)(128)(2,1)S(1)}, bf16[96]{0:T(256)(128)(2,1)S(1)}, bf16[9...) all-reduce(bf16[96]{0:T(256)(128)(2,1)S(1)} %dynamic-slice.9, ...), channel_id=1, replica_groups=mesh['ctx'=4,'wsh'=8] {'ctx'}, use_global_device_ids=true, to_apply=%region_19.20 | all-reduce | flops 1152 | bytes 4608 | tf_op jit(solution)/shard_map/psum | solution.py:272
  780.9 6.4 add_bitcast_fusion
  787.3 18.7 %all-reduce.23.cloned.1.call-done = (bf16[96,2304]{0,1:T(8,128)(2,1)}, bf16[96,768]{1,0:T(8,128)(2,1)}, bf16[96,3072]{1,0:T(8,128)(2,1)}, bf16[384,768]{1,0:T(8,128)(2,1)}) async-done(((bf16[96,2304]{0,1:T(8,128)(2,1)}, bf16[96,768]{1,0:T(8,128)(2,1)}, bf16[96,3072]{1,0:T(8,128)(2,1)}, bf16[384,768]{1,0:T(8,128)(2,1)}), (bf16[96,2304]{0,1:T(8,128)(2,1)}, bf16[96,768]{1,0:T(8,128)(2,1)}, ...) | async-done | bytes 1769488 | tf_op jit(solution)/shard_map/psum | solution.py:271
  806.0 2.3 copy.102
  808.3 1.6 convert_element_type.240
  809.9 2.2 convert_element_type.247
  (160 shorter events, 37.1 us)
Async XLA Ops:
  7.2 47.3 %all-gather.8.cloned.1.call-start = ((), (), s32[]{:S(2)}) async-start(), calls=%async_computation.6 | async-start | bytes 3981312 | tf_op jit(solution)/shard_map/all_gather | solution.py:79
  7.9 147.6 %all-gather.10.cloned.1.call-start = ((), (), s32[]{:S(2)}) async-start(), calls=%async_computation.7 | async-start | bytes 11796480 | tf_op jit(solution)/shard_map/all_gather | solution.py:110
  47.5 13.4 %copy-start.15 = (s32[1,512]{1,0:T(1,128)S(1)}, s32[1,512]{1,0:T(1,128)}, u32[]{:S(2)}) copy-start(s32[1,512]{1,0:T(1,128)} %param.17) | copy-start | bytes 6148
  60.1 119.7 %all-gather.12.cloned.1.call-start = ((), (), s32[]{:S(2)}) async-start(), calls=%async_computation.8 | async-start | bytes 1327104 | tf_op jit(solution)/shard_map/all_gather | solution.py:82
  60.8 169.7 %reduce-scatter.9.cloned.1.call-start = ((), (), s32[]{:S(2)}) async-start(), calls=%async_computation.9 | async-start | bytes 3932160 | tf_op jit(solution)/shard_map/reduce_scatter | solution.py:135
  169.8 1.8 copy-start.5
  171.1 1.1 copy-start.7
  172.3 1.8 copy-start.12
  173.1 2.0 copy-start
  175.7 6.2 copy-start.11
  181.9 5.9 copy-start.16
  181.9 48.6 %copy-start.2 = (bf16[1,512,768]{2,1,0:T(8,128)(2,1)S(1)}, bf16[1,512,768]{2,1,0:T(8,128)(2,1)}, u32[]{:S(2)}) copy-start(bf16[1,512,768]{2,1,0:T(8,128)(2,1)} %param.16) | copy-start | bytes 2359300
  186.7 97.1 %all-gather.14.cloned.1.call-start = ((), (), s32[]{:S(2)}) async-start(), calls=%async_computation.10 | async-start | bytes 5308416 | tf_op jit(solution)/shard_map/all_gather | solution.py:86
  187.2 148.6 %all-gather.16.cloned.1.call-start = ((), (), s32[]{:S(2)}) async-start(), calls=%async_computation.11 | async-start | bytes 5308416 | tf_op jit(solution)/shard_map/all_gather | solution.py:88
  187.8 210.6 %all-gather.18.cloned.1.call-start = ((), (), s32[]{:S(2)}) async-start(), calls=%async_computation.12 | async-start | bytes 3932160 | tf_op jit(solution)/shard_map/all_gather | solution.py:168
  230.6 53.2 %copy-start.3 = (bf16[512,768]{1,0:T(8,128)(2,1)S(1)}, bf16[512,768]{1,0:T(8,128)(2,1)}, u32[]{:S(2)}) copy-start(bf16[512,768]{1,0:T(8,128)(2,1)} %reduce-scatter.9.cloned.1.call-done) | copy-start | bytes 2359300
  335.8 6.6 copy-start.4
  335.8 8.0 copy-start.20
  342.4 2.4 copy-start.17
  343.2 6.4 slice-start
  343.8 5.8 copy-start.10
  344.8 4.8 slice-start.1
  349.6 3.3 copy-start.19
  352.8 1.1 copy-start.9
  355.5 179.3 %reduce-scatter.11.cloned.1.call-start = ((), (), s32[]{:S(2)}) async-start(), calls=%async_computation.13 | async-start | bytes 11796480 | tf_op jit(solution)/shard_map/reduce_scatter | solution.py:209
  412.0 3.8 copy-start.1
  412.0 3.8 copy-start.13
  417.1 1.2 copy-start.6
  418.3 1.1 copy-start.8
  439.6 150.5 %reduce-scatter.19.cloned.1.call-start = ((), (), s32[]{:S(2)}) async-start(), calls=%async_computation.17 | async-start | bytes 3981312
  546.1 78.2 %reduce-scatter.13.cloned.1.call-start = ((), (), s32[]{:S(2)}) async-start(), calls=%async_computation.14 | async-start | bytes 1327104 | tf_op jit(solution)/shard_map/reduce_scatter | solution.py:225
  549.5 130.3 %reduce-scatter.15.cloned.1.call-start = ((), (), s32[]{:S(2)}) async-start(), calls=%async_computation.15 | async-start | bytes 5308416 | tf_op jit(solution)/shard_map/reduce_scatter | solution.py:237
  556.0 179.4 %reduce-scatter.17.cloned.1.call-start = ((), (), s32[]{:S(2)}) async-start(), calls=%async_computation.16 | async-start | bytes 5308416 | tf_op jit(solution)/shard_map/reduce_scatter | solution.py:243
  563.5 174.5 %copy-start.18 = (bf16[96]{0:T(256)(128)(2,1)S(1)}, bf16[96]{0:T(256)(128)(2,1)}, u32[]{:S(2)}) copy-start(bf16[96]{0:T(256)(128)(2,1)} %param.30) | copy-start | bytes 580
  563.5 242.5 %all-reduce.23.cloned.1.call-start = ((), (), s32[]{:S(2)}) async-start(), calls=%async_computation.18 | async-start | bytes 3833856 | tf_op jit(solution)/shard_map/psum | solution.py:271
  806.0 6.1 copy-start.14
Sparse Core Ops, SparseCore 0:
  9.7 44.7 all-gather.7
  60.2 95.2 all-gather.9
  157.1 22.6 all-gather.11
  186.8 43.7 reduce-scatter.8
  232.0 51.6 all-gather.13
  285.2 50.5 all-gather.15
  355.6 42.7 all-gather.17
  439.8 95.0 reduce-scatter.10
  546.2 43.8 reduce-scatter.18
  592.9 31.3 reduce-scatter.12
  626.8 52.9 reduce-scatter.14
  682.1 53.3 reduce-scatter.16
  739.9 66.0 all-reduce.22
where the time goes:
time: 825 us; the launch traced here: 820 us
  waiting for transfers between devices  547 us (66%)
  matrix products  82 us (10%)
  blocking collectives  80.7 us (10%)
  local copies, waits for them, and re-layouts  68.7 us (8%)
  other arithmetic  24.3 us (3%)
  between operations  16.7 us (2%)
    reduce_scatter x1, waiting for transfers between devices, on_device(): lax.psum_scatter(spread_grad, 'ctx', scatter_dimension=0, tiled=True)  95.1 us
    all_gather x1, waiting for transfers between devices, on_device(): group_qkv = lax.all_gather(own_qkv, 'ctx', axis=0, tiled=True)  94.4 us
    unnamed x2, blocking collectives  57.6 us
    reduce_scatter x1, waiting for transfers between devices, on_device(): lax.psum_scatter(grad_down_w.astype(jnp.bfloat16), 'wsh', scatter_dimensi...  55.6 us
    reduce_scatter x1, waiting for transfers between devices, on_device(): lax.psum_scatter(grad_up_w.astype(jnp.bfloat16), 'wsh', scatter_dimension...  55.5 us
    all_gather x1, waiting for transfers between devices, on_device(): lax.all_gather(up_weight, 'wsh', axis=0, tiled=True)  50.2 us
    all_gather x1, waiting for transfers between devices, on_device(): group_grads = lax.all_gather(grad_attended, 'ctx', axis=0, tiled=True)  42.9 us
    all_gather x1, waiting for transfers between devices, on_device(): lax.all_gather(down_weight, 'wsh', axis=0, tiled=True)  32.7 us
  transfers between devices with their start and end apart: 13, of which 13 were waited for; matrix products, arithmetic and copies ran while one was open for 10% of the time, Pallas kernels for 0%

commit v1 on v0

--- a/solution.py
+++ b/solution.py
@@ -107,7 +107,12 @@
     own_qkv = (jnp.dot(inputs, whole_qkv, preferred_element_type=jnp.float32) + qkv_shift).astype(
         jnp.bfloat16
     )
-    group_qkv = lax.all_gather(own_qkv, "ctx", axis=0, tiled=True)
+    ring = [own_qkv]
+    for hop in range(3):
+        ring.append(lax.ppermute(ring[-1], "ctx", [(dev, (dev + 1) % 4) for dev in range(4)]))
+    group_qkv = jnp.roll(
+        jnp.concatenate(ring[::-1], axis=0), (lax.axis_index("ctx") + 1) * ring[0].shape[0], axis=0
+    )
     picked = jnp.take(group_qkv, order, axis=0)
     query = picked[:, :width].reshape(blocks, CLUSTER, heads, HEAD_DIM)
     keyed = picked[:, width : 2 * width].reshape(blocks, CLUSTER, heads, HEAD_DIM)

time: 825 us -> 911 us (1.10)
  waiting for transfers between devices: 547 us -> 604 us
  local copies, waits for them, and re-layouts: 68.7 us -> 95.1 us
    ppermute x0 -> x3, waiting for transfers between devices: none -> 158 us  [on_device(): lax.ppermute(ring[-1], 'ctx', [(dev, (dev + 1) % 4) for dev in range(4)])]
    all_gather x1 -> x0, waiting for transfers between devices: 94.4 us -> none  [on_device(): group_qkv = lax.all_gather(own_qkv, 'ctx', axis=0, tiled=True)]
    unnamed x79 -> x92, local copies, waits for them, and re-layouts: 22 us -> 39.8 us
    unnamed x14 -> x13, waiting for transfers between devices: 29.1 us -> 28.3 us
  transfers between devices with their start and end apart: 13 -> 15, of which waited for: 13 -> 14; matrix products, arithmetic and copies ran while one was open for 10% -> 12% of each run, Pallas kernels for 0% -> 0%
where the time goes in v1:
time: 911 us; the launch traced here: 904 us
  waiting for transfers between devices  604 us (66%)
  local copies, waits for them, and re-layouts  95.1 us (10%)
  matrix products  81.1 us (9%)
  blocking collectives  80.7 us (9%)
  other arithmetic  22.7 us (2%)
  between operations  17.2 us (2%)
    ppermute x3, waiting for transfers between devices, on_device(): lax.ppermute(ring[-1], 'ctx', [(dev, (dev + 1) % 4) for dev in range(4)])  158 us
    reduce_scatter x1, waiting for transfers between devices, on_device(): lax.psum_scatter(spread_grad, 'ctx', scatter_dimension=0, tiled=True)  95.1 us
    unnamed x2, blocking collectives  57.6 us
    reduce_scatter x1, waiting for transfers between devices, on_device(): lax.psum_scatter(grad_up_w.astype(jnp.bfloat16), 'wsh', scatter_dimension...  55.8 us
    reduce_scatter x1, waiting for transfers between devices, on_device(): lax.psum_scatter(grad_down_w.astype(jnp.bfloat16), 'wsh', scatter_dimensi...  55.3 us
    all_gather x1, waiting for transfers between devices, on_device(): lax.all_gather(up_weight, 'wsh', axis=0, tiled=True)  50.2 us
    all_gather x1, waiting for transfers between devices, on_device(): group_grads = lax.all_gather(grad_attended, 'ctx', axis=0, tiled=True)  42.9 us
    unnamed x92, local copies, waits for them, and re-layouts  39.8 us
  transfers between devices with their start and end apart: 15, of which 14 were waited for; matrix products, arithmetic and copies ran while one was open for 12% of the time, Pallas kernels for 0%

profile of v1, /device:TPU:0, one launch (start us, length us, event | category | flops | bytes accessed | tf_op | source)
XLA Modules:
  0.0 903.9 jit_solution(13826586290666783661)
XLA Ops:
  15.8 31.6 %all-reduce.18 = (bf16[768]{0:T(1024)(128)(2,1)S(1)}, bf16[768]{0:T(1024)(128)(2,1)S(1)}, bf16[768]{0:T(1024)(128)(2,1)S(1)}, bf16[768]{0:T(1024)(128)(2,1)S(1)}...) all-reduce(bf16[768]{0:T(1024)(128)(2,1)S(1)} %dynamic-update-slice, ...), channel_id=1, replica_groups=mesh['ctx'=4,'wsh'=8] {'wsh'}, use_global_device_ids=true, to_apply=%add.1 | all-reduce | flops 5376 | bytes 21504
  47.5 7.0 all-gather.7.cloned.1.call-done
  54.4 4.2 fusion.18
  60.2 52.8 %collective-permute-done = bf16[512,2304]{1,0:T(8,128)(2,1)S(1)} collective-permute-done((bf16[512,2304]{1,0:T(8,128)(2,1)S(1)}, bf16[512,2304]{1,0:T(8,128)(2,1)S(1)}, u32[]{:S(2)}, u32[]{:S(2)}) %collective-permute-start) | collective-permute-done | bytes 2359328 | tf_op jit(solution)/shard_map/ppermute | solution.py:112
  115.1 53.0 %collective-permute-done.1 = bf16[512,2304]{1,0:T(8,128)(2,1)} collective-permute-done((bf16[512,2304]{1,0:T(8,128)(2,1)S(1)}, bf16[512,2304]{1,0:T(8,128)(2,1)}, u32[]{:S(2)}, u32[]{:S(2)}) %collective-permute-start.1) | collective-permute-done | bytes 2359328 | tf_op jit(solution)/shard_map/ppermute | solution.py:112
  168.4 52.6 %collective-permute-done.2 = bf16[512,2304]{1,0:T(8,128)(2,1)} collective-permute-done((bf16[512,2304]{1,0:T(8,128)(2,1)}, bf16[512,2304]{1,0:T(8,128)(2,1)}, u32[]{:S(2)}, u32[]{:S(2)}) %collective-permute-start.2) | collective-permute-done | bytes 2359328 | tf_op jit(solution)/shard_map/ppermute | solution.py:112
  221.0 3.3 constant_dynamic-update-slice_fusion.7
  224.3 3.4 constant_dynamic-update-slice_fusion.6
  229.2 1.7 constant_dynamic-update-slice_fusion.4
  230.9 3.2 constant_dynamic-update-slice_fusion.3
  234.1 3.2 constant_dynamic-update-slice_fusion.2
  240.5 7.9 constant_dynamic-slice_fusion
  248.4 10.0 %gather_fusion = bf16[512,2304]{1,0:T(8,128)(2,1)S(1)} fusion(bf16[2048,2304]{1,0:T(8,128)(2,1)} %constant_dynamic-slice_fusion, s32[1024]{0:T(1024)S(1)} %pad_clamp_fusion), kind=kCustom, calls=%fused_computation | custom fusion | bytes 4720640 | tf_op jit(solution)/shard_map/jit(_take)/gather | solution.py:116
  266.2 2.3 add_convert_fusion.1
  268.6 4.7 scatter_custom_fusion
  274.5 13.2 %all-gather = bf16[8,1,384]{2,1,0:T(2,128)(2,1)S(1)} all-gather(bf16[1,1,384]{2,1,0:T(2,128)(2,1)S(1)} %reshape.219), channel_id=1, replica_groups=mesh['ctx'=4,'wsh'=8] {'wsh'}, dimensions={0}, use_global_device_ids=true | all-gather | bytes 6912 | tf_op jit(solution)/shard_map/all_gather | solution.py:87
  287.7 27.7 %reduce-scatter.9.cloned.1.call-done = bf16[512,768]{1,0:T(8,128)(2,1)} async-done(((bf16[2048,768]{1,0:T(8,128)(2,1)}), bf16[512,768]{1,0:T(8,128)(2,1)}) %reduce-scatter.9.cloned.1.call-update) | async-done | bytes 786448 | tf_op jit(solution)/shard_map/reduce_scatter | solution.py:140
  318.4 50.2 %all-gather.11.cloned.1.call-done = bf16[768,3072]{1,0:T(8,128)(2,1)} async-done(((bf16[96,3072]{1,0:T(8,128)(2,1)}), bf16[768,3072]{1,0:T(8,128)(2,1)}) %all-gather.11.cloned.1.call-update) | async-done | bytes 4718608 | tf_op jit(solution)/shard_map/all_gather | solution.py:86
  368.6 19.3 %fusion.2 = (bf16[512,3072]{1,0:T(8,128)(2,1)}, f32[512,3072]{1,0:T(8,128)}) fusion(f32[3072]{0:T(1024)S(1)} %bitcast.121, bf16[768,3072]{1,0:T(8,128)(2,1)} %all-gather.11.cloned.1.call-done, f32[768]{0:T(1024)S(1)} %convert_element_type.212, f32[768]{0:T(1024)S(1)} %convert_element_type.211, f32[512]{0:T(512)S(1)} %add_rsqrt_fusion.1, ...), kind=kOutput, calls=%fused_computation.8 | convolution fusion | flops 2522873856 | bytes 15751168 | tf_op jit(solution)/shard_map/dot_general | solution.py:145
  387.9 32.7 %all-gather.13.cloned.1.call-done = bf16[3072,768]{1,0:T(8,128)(2,1)} async-done(((bf16[384,768]{1,0:T(8,128)(2,1)}), bf16[3072,768]{1,0:T(8,128)(2,1)}) %all-gather.13.cloned.1.call-update) | async-done | bytes 4718608 | tf_op jit(solution)/shard_map/all_gather | solution.py:88
  420.6 6.3 fusion.87
  429.7 4.7 fusion.90
  434.4 3.2 multiply_reduce_fusion.1
  440.4 42.9 %all-gather.15.cloned.1.call-done = bf16[2048,768]{1,0:T(8,128)(2,1)} async-done(((bf16[512,768]{1,0:T(8,128)(2,1)}), bf16[2048,768]{1,0:T(8,128)(2,1)}) %all-gather.15.cloned.1.call-update) | async-done | bytes 3145744 | tf_op jit(solution)/shard_map/all_gather | solution.py:173
  483.3 5.5 gather_fusion.1
  488.8 3.2 convolution_convert_fusion.4
  492.1 2.3 copy.89
  494.4 2.4 reshape.158
  496.8 3.8 multiply_reduce_fusion
  508.9 4.3 copy.101
  513.2 10.6 %scatter_custom_fusion.1 = bf16[2048,2304]{1,0:T(8,128)(2,1)} fusion(s32[512]{0:T(512)S(1)} %bitcast.125, bf16[512,2304]{1,0:T(8,128)(2,1)} %copy.101, bf16[]{:T(256)} %constant.46.clone.1), kind=kCustom, calls=%fused_computation.34 | custom fusion | bytes 9437696 | tf_op jit(solution)/shard_map/scatter | solution.py:212
  523.9 95.1 %reduce-scatter.11.cloned.1.call-done = bf16[512,2304]{1,0:T(8,128)(2,1)} async-done(((bf16[2048,2304]{1,0:T(8,128)(2,1)}), bf16[512,2304]{1,0:T(8,128)(2,1)}) %reduce-scatter.11.cloned.1.call-update) | async-done | bytes 2359312 | tf_op jit(solution)/shard_map/reduce_scatter | solution.py:214
  619.0 5.5 fusion.19
  624.6 5.8 copy.107
  630.4 3.3 convolution_convert_fusion.3
  634.0 7.2 convolution_convert_fusion
  641.3 6.5 convolution_convert_fusion.1
  647.9 26.4 %reduce-scatter.19.cloned.1.call-done = bf16[96,2304]{1,0:T(8,128)(2,1)} async-done(((bf16[768,2304]{1,0:T(8,128)(2,1)}), bf16[96,2304]{1,0:T(8,128)(2,1)}) %reduce-scatter.19.cloned.1.call-update) | async-done | bytes 442384
  674.3 2.1 copy.108
  676.4 32.3 %reduce-scatter.13.cloned.1.call-done = bf16[96,768]{1,0:T(8,128)(2,1)} async-done(((bf16[768,768]{1,0:T(8,128)(2,1)}), bf16[96,768]{1,0:T(8,128)(2,1)}) %reduce-scatter.13.cloned.1.call-update) | async-done | bytes 147472 | tf_op jit(solution)/shard_map/reduce_scatter | solution.py:230
  708.7 55.3 %reduce-scatter.17.cloned.1.call-done = bf16[384,768]{1,0:T(8,128)(2,1)} async-done(((bf16[3072,768]{1,0:T(8,128)(2,1)}), bf16[384,768]{1,0:T(8,128)(2,1)}) %reduce-scatter.17.cloned.1.call-update) | async-done | bytes 589840 | tf_op jit(solution)/shard_map/reduce_scatter | solution.py:248
  764.0 55.8 %reduce-scatter.15.cloned.1.call-done = bf16[96,3072]{1,0:T(8,128)(2,1)} async-done(((bf16[768,3072]{1,0:T(8,128)(2,1)}), bf16[96,3072]{1,0:T(8,128)(2,1)}) %reduce-scatter.15.cloned.1.call-update) | async-done | bytes 589840 | tf_op jit(solution)/shard_map/reduce_scatter | solution.py:242
  822.8 26.0 %all-reduce.17 = (bf16[768]{0:T(1024)(128)(2,1)S(1)}, bf16[768]{0:T(1024)(128)(2,1)S(1)}, bf16[768]{0:T(1024)(128)(2,1)S(1)}, bf16[768]{0:T(1024)(128)(2,1)S(1)}...) all-reduce(bf16[768]{0:T(1024)(128)(2,1)S(1)} %dynamic-update-slice, ...), channel_id=1, replica_groups=mesh['ctx'=4,'wsh'=8] {'wsh'}, use_global_device_ids=true, to_apply=%add.7 | all-reduce | flops 9984 | bytes 39936
  849.5 9.9 %all-reduce.19 = (bf16[96]{0:T(256)(128)(2,1)S(1)}, bf16[96]{0:T(256)(128)(2,1)S(1)}, bf16[96]{0:T(256)(128)(2,1)S(1)}, bf16[96]{0:T(256)(128)(2,1)S(1)}, bf16[9...) all-reduce(bf16[96]{0:T(256)(128)(2,1)S(1)} %dynamic-slice.9, ...), channel_id=1, replica_groups=mesh['ctx'=4,'wsh'=8] {'ctx'}, use_global_device_ids=true, to_apply=%region_19.20 | all-reduce | flops 1152 | bytes 4608 | tf_op jit(solution)/shard_map/psum | solution.py:277
  865.3 6.4 add_bitcast_fusion
  871.7 18.6 %all-reduce.23.cloned.1.call-done = (bf16[96,2304]{0,1:T(8,128)(2,1)}, bf16[96,768]{1,0:T(8,128)(2,1)}, bf16[96,3072]{1,0:T(8,128)(2,1)}, bf16[384,768]{1,0:T(8,128)(2,1)}) async-done(((bf16[96,2304]{0,1:T(8,128)(2,1)}, bf16[96,768]{1,0:T(8,128)(2,1)}, bf16[96,3072]{1,0:T(8,128)(2,1)}, bf16[384,768]{1,0:T(8,128)(2,1)}), (bf16[96,2304]{0,1:T(8,128)(2,1)}, bf16[96,768]{1,0:T(8,128)(2,1)}, ...) | async-done | bytes 1769488 | tf_op jit(solution)/shard_map/psum | solution.py:276
  890.3 2.2 convert_element_type.247
  892.5 2.2 convert_element_type.250
  (178 shorter events, 52.7 us)
Async XLA Ops:
  7.2 47.2 %all-gather.7.cloned.1.call-start = ((), (), s32[]{:S(2)}) async-start(), calls=%async_computation.6 | async-start | bytes 3981312 | tf_op jit(solution)/shard_map/all_gather | solution.py:79
  7.9 258.3 %all-gather.9.cloned.1.call-start = ((), (), s32[]{:S(2)}) async-start(), calls=%async_computation.7 | async-start | bytes 1327104 | tf_op jit(solution)/shard_map/all_gather | solution.py:82
  47.5 120.8 %copy-start.18 = (s32[1,512]{1,0:T(1,128)S(1)}, s32[1,512]{1,0:T(1,128)}, u32[]{:S(2)}) copy-start(s32[1,512]{1,0:T(1,128)} %param.17) | copy-start | bytes 6148
  58.7 54.3 %collective-permute-start = (bf16[512,2304]{1,0:T(8,128)(2,1)S(1)}, bf16[512,2304]{1,0:T(8,128)(2,1)S(1)}, u32[]{:S(2)}, u32[]{:S(2)}) collective-permute-start(bf16[512,2304]{1,0:T(8,128)(2,1)S(1)} %fusion.18), channel_id=1, source_target_pairs={{0,8},{8,16},{16,24},{24,0},{1,9},{9,17},{17,25},{25,1},{2,10},{10... | collective-permute-start | bytes 7077896 | tf_op jit(solution)/shard_map/ppermute | solution.py:112
  113.0 1.5 copy-start.2
  114.6 53.6 %collective-permute-start.1 = (bf16[512,2304]{1,0:T(8,128)(2,1)S(1)}, bf16[512,2304]{1,0:T(8,128)(2,1)}, u32[]{:S(2)}, u32[]{:S(2)}) collective-permute-start(bf16[512,2304]{1,0:T(8,128)(2,1)S(1)} %collective-permute-done), channel_id=1, source_target_pairs={{0,8},{8,16},{16,24},{24,0},{1,9},{9,17},{17,25},{25,1},{2,10},{10... | collective-permute-start | bytes 7077896 | tf_op jit(solution)/shard_map/ppermute | solution.py:112
  168.1 52.9 %collective-permute-start.2 = (bf16[512,2304]{1,0:T(8,128)(2,1)}, bf16[512,2304]{1,0:T(8,128)(2,1)}, u32[]{:S(2)}, u32[]{:S(2)}) collective-permute-start(bf16[512,2304]{1,0:T(8,128)(2,1)} %collective-permute-done.1), channel_id=1, source_target_pairs={{0,8},{8,16},{16,24},{24,0},{1,9},{9,17},{17,25},{25,1},{2,10},{10... | collective-permute-start | bytes 7077896 | tf_op jit(solution)/shard_map/ppermute | solution.py:112
  168.2 147.2 %reduce-scatter.9.cloned.1.call-start = ((), (), s32[]{:S(2)}) async-start(), calls=%async_computation.8 | async-start | bytes 3932160 | tf_op jit(solution)/shard_map/reduce_scatter | solution.py:140
  224.3 3.4 copy-start.3
  260.2 1.8 copy-start.7
  261.5 1.1 copy-start.9
  262.7 1.8 copy-start.14
  263.5 2.0 copy-start
  266.1 2.4 copy-start.13
  268.6 5.9 copy-start.19
  268.6 46.8 %copy-start.4 = (bf16[1,512,768]{2,1,0:T(8,128)(2,1)S(1)}, bf16[1,512,768]{2,1,0:T(8,128)(2,1)}, u32[]{:S(2)}) copy-start(bf16[1,512,768]{2,1,0:T(8,128)(2,1)} %param.16) | copy-start | bytes 2359300
  273.3 95.3 %all-gather.11.cloned.1.call-start = ((), (), s32[]{:S(2)}) async-start(), calls=%async_computation.9 | async-start | bytes 5308416 | tf_op jit(solution)/shard_map/all_gather | solution.py:86
  273.8 146.8 %all-gather.13.cloned.1.call-start = ((), (), s32[]{:S(2)}) async-start(), calls=%async_computation.10 | async-start | bytes 5308416 | tf_op jit(solution)/shard_map/all_gather | solution.py:88
  274.4 208.9 %all-gather.15.cloned.1.call-start = ((), (), s32[]{:S(2)}) async-start(), calls=%async_computation.11 | async-start | bytes 3932160 | tf_op jit(solution)/shard_map/all_gather | solution.py:173
  315.4 53.2 %copy-start.5 = (bf16[512,768]{1,0:T(8,128)(2,1)S(1)}, bf16[512,768]{1,0:T(8,128)(2,1)}, u32[]{:S(2)}) copy-start(bf16[512,768]{1,0:T(8,128)(2,1)} %reduce-scatter.9.cloned.1.call-done) | copy-start | bytes 2359300
  420.6 6.6 copy-start.6
  420.6 8.0 copy-start.23
  427.2 2.4 copy-start.20
  428.0 6.4 slice-start
  428.6 5.8 copy-start.12
  429.7 4.8 slice-start.1
  434.4 3.3 copy-start.22
  437.7 1.1 copy-start.11
  440.4 178.7 %reduce-scatter.11.cloned.1.call-start = ((), (), s32[]{:S(2)}) async-start(), calls=%async_computation.12 | async-start | bytes 11796480 | tf_op jit(solution)/shard_map/reduce_scatter | solution.py:214
  496.8 3.8 copy-start.1
  496.8 3.8 copy-start.15
  502.0 1.2 copy-start.8
  503.2 1.2 copy-start.10
  523.8 150.5 %reduce-scatter.19.cloned.1.call-start = ((), (), s32[]{:S(2)}) async-start(), calls=%async_computation.16 | async-start | bytes 3981312
  630.4 78.3 %reduce-scatter.13.cloned.1.call-start = ((), (), s32[]{:S(2)}) async-start(), calls=%async_computation.13 | async-start | bytes 1327104 | tf_op jit(solution)/shard_map/reduce_scatter | solution.py:230
  633.7 130.3 %reduce-scatter.17.cloned.1.call-start = ((), (), s32[]{:S(2)}) async-start(), calls=%async_computation.15 | async-start | bytes 5308416 | tf_op jit(solution)/shard_map/reduce_scatter | solution.py:248
  641.3 178.5 %reduce-scatter.15.cloned.1.call-start = ((), (), s32[]{:S(2)}) async-start(), calls=%async_computation.14 | async-start | bytes 5308416 | tf_op jit(solution)/shard_map/reduce_scatter | solution.py:242
  647.8 174.6 %copy-start.21 = (bf16[96]{0:T(256)(128)(2,1)S(1)}, bf16[96]{0:T(256)(128)(2,1)}, u32[]{:S(2)}) copy-start(bf16[96]{0:T(256)(128)(2,1)} %param.30) | copy-start | bytes 580
  647.8 242.4 %all-reduce.23.cloned.1.call-start = ((), (), s32[]{:S(2)}) async-start(), calls=%async_computation.17 | async-start | bytes 3833856 | tf_op jit(solution)/shard_map/psum | solution.py:276
  890.3 4.4 copy-start.16
  890.3 5.6 copy-start.17
Sparse Core Ops, SparseCore 0:
  9.7 44.7 all-gather.6
  168.3 22.2 all-gather.8
  273.4 41.9 reduce-scatter.8
  316.9 51.6 all-gather.10
  370.1 50.5 all-gather.12
  440.5 42.7 all-gather.14
  524.0 95.0 reduce-scatter.10
  630.5 43.8 reduce-scatter.18
  677.3 31.3 reduce-scatter.12
  711.0 53.0 reduce-scatter.16
  766.4 53.3 reduce-scatter.14
  824.1 66.0 all-reduce.22
